TPU v7x, 256 devices: a whole 4x4x8 slice. The times are simulated.
256 devices in a mesh: row: 16 (over z_hi, y), col: 16 (over z_lo, x, core).
Axes of the slice: x: 4, y: 4, z: 8 (z_hi: 4, z_lo: 2; z = z_hi * 2 + z_lo), core: 2. Of those that a mesh axis runs over, the one named last changes fastest.
Arguments:
- right_side: float32 [16, 16, 1024, 256], P('row', 'col'), may hold values from -4 to 4
- local_operator: bfloat16 [16, 16, 1536, 1536], P('row', 'col'), may hold values from -1 to 4
- local_inverse: bfloat16 [16, 16, 1536, 1536], P('row', 'col'), may hold values from -1 to 1
- coarse_basis: bfloat16 [16, 16, 1536, 32], P('row', 'col'), may hold values from -1 to 1
- coarse_inverse: bfloat16 [16, 512, 8192], P(None, 'col', 'row'), may hold values from -1 to 1
- send_rows: int32 [16, 16, 4, 128], P('row', 'col'), may hold values from 0 to 1023, as said below
- send_count: int32 [16, 16, 4], P('row', 'col'), may hold values from 0 to 128, as said below
Outputs:
- solution: float32 [16, 16, 1024, 256], P('row', 'col')
Inputs may be any that keep to these rules, and one draw needn't show every extreme that they name: `send_rows`: within one subdomain and direction the entries are distinct owned rows; entries at or past that direction's count are ignored. `send_count`: 0 exactly where the neighbour in that direction lies outside the grid of subdomains; otherwise from 128 // 4 to 128, and 128 is reached.
All inputs are finite; a program needn't handle non-finite values.
Results may differ from a plain program's by a relative error of at most 0.023.
Values may be sent and summed in bfloat16 or wider, within the bound.
A program may use at most 64 MiB of HBM per device.

v0:
```python
import jax
import jax.numpy as jnp
from jax import lax
from jax.sharding import PartitionSpec as P

ITERS = 3
DAMPING = 0.5


def passed_along(shard, axis, by):
    devices = lax.axis_size(axis)
    pairs = [(i, i + by) for i in range(devices) if 0 <= i + by < devices]
    return lax.ppermute(shard, axis, pairs)


def ghost_trade(buffer):
    arrived = []
    for offset, source in ((1, 1), (-1, 0)):
        arrived.append(passed_along(buffer[source], "row", offset))
    for offset, source in ((1, 3), (-1, 2)):
        arrived.append(passed_along(buffer[source], "col", offset))
    return jnp.stack(arrived)


def per_device(
    right_side, local_operator, local_inverse, coarse_basis, coarse_inverse, send_rows, send_count
):
    target = right_side[0, 0]
    operator = local_operator[0, 0]
    inverse = local_inverse[0, 0]
    prolong = coarse_basis[0, 0]
    rows_list = send_rows[0, 0]
    counts = send_count[0, 0]
    own_rows, columns = target.shape
    tile_rows = rows_list.shape[1]
    live_mask = (lax.broadcasted_iota(jnp.int32, rows_list.shape, 1) < counts[:, None]).astype(
        jnp.float32
    )
    live_half = live_mask[..., None].astype(jnp.bfloat16)
    flat_rows = rows_list.reshape(-1)
    coarse_rows = coarse_inverse.reshape(-1, coarse_inverse.shape[2])

    def with_ghosts(values_half):
        packed = values_half[flat_rows].reshape(4, tile_rows, columns) * live_half
        ghosts = ghost_trade(packed)
        return jnp.concatenate([values_half, ghosts.reshape(4 * tile_rows, columns)], axis=0)

    def owner_sum(local_terms):
        rim_half = local_terms[own_rows:].astype(jnp.bfloat16).reshape(4, tile_rows, columns)
        returned = ghost_trade(rim_half)
        weighted = returned.astype(jnp.float32) * live_mask[..., None]
        summed = (
            jnp.zeros((own_rows, columns), jnp.float32)
            .at[flat_rows]
            .add(weighted.reshape(-1, columns))
        )
        return local_terms[:own_rows] + summed

    solution = jnp.zeros((own_rows, columns), jnp.float32)
    for sweep in range(ITERS):
        if sweep == 0:
            residual_half = target.astype(jnp.bfloat16)
        else:
            solution_half = solution.astype(jnp.bfloat16)
            image = owner_sum(
                jnp.dot(operator, with_ghosts(solution_half), preferred_element_type=jnp.float32)
            )
            residual_half = (target - image).astype(jnp.bfloat16)
        residual_local = with_ghosts(residual_half)
        local_part = jnp.dot(inverse, residual_local, preferred_element_type=jnp.float32)
        restricted = lax.dot_general(
            prolong, residual_local, (((0,), (0,)), ((), ())), preferred_element_type=jnp.float32
        )
        restricted = restricted.astype(jnp.bfloat16)
        block_rows = lax.all_gather(restricted, "col", axis=0, tiled=True)
        solved = lax.psum_scatter(
            jnp.dot(coarse_rows, block_rows, preferred_element_type=jnp.float32).astype(
                jnp.bfloat16
            ),
            "row",
            scatter_dimension=0,
            tiled=True,
        )
        update = owner_sum(
            local_part + jnp.dot(prolong, solved, preferred_element_type=jnp.float32)
        )
        solution = solution + DAMPING * update
    return solution[None, None]


def solution(mesh):
    return jax.shard_map(
        per_device,
        mesh=mesh,
        in_specs=(
            P("row", "col", None, None),
            P("row", "col", None, None),
            P("row", "col", None, None),
            P("row", "col", None, None),
            P(None, "col", "row"),
            P("row", "col", None, None),
            P("row", "col", None),
        ),
        out_specs=P("row", "col", None, None),
        check_vma=False,
    )
```

profile of v0, /device:TPU:89, one launch (start us, length us, event | category | flops | bytes accessed | tf_op | source)
XLA Modules:
  0.0 582.0 jit_solution(5471875140377850859)
XLA Ops:
  11.4 5.8 collective-permute-start
  20.1 3.0 collective-permute-start.2
  25.1 8.6 %collective-permute-done.1 = bf16[128,256]{1,0:T(8,128)(2,1)S(1)} collective-permute-done((bf16[128,256]{1,0:T(8,128)(2,1)S(1)}, bf16[128,256]{1,0:T(8,128)(2,1)S(1)}, u32[]{:S(2)}, u32[]{:S(2)}) %collective-permute-start.1) | collective-permute-done | bytes 65568 | tf_op jit(solution)/shard_map/ppermute | solution.py:13
  33.9 19.0 %all_gather.9 = bf16[512,256]{1,0:T(8,128)(2,1)S(1)} all-gather(bf16[32,256]{1,0:T(8,128)(2,1)S(1)} %fusion.22), channel_id=1, replica_groups=mesh['row'=16,'col'=16] {'col'}, dimensions={0}, use_global_device_ids=true | all-gather | bytes 278528 | tf_op jit(solution)/shard_map/all_gather | solution.py:75
  54.3 3.8 fusion.8
  58.0 75.6 %reduce-scatter.10.cloned.1.call-done = bf16[32,256]{1,0:T(8,128)(2,1)} async-done(((bf16[512,256]{1,0:T(8,128)(2,1)}), bf16[32,256]{1,0:T(8,128)(2,1)}) %reduce-scatter.10.cloned.1.call-update) | async-done | bytes 16400
  134.8 4.5 collective-permute-start.4
  139.3 5.0 collective-permute-start.7
  144.3 3.0 collective-permute-start.6
  149.7 9.0 %collective-permute-done.5 = bf16[128,256]{0,1:T(8,128)(2,1)S(1)} collective-permute-done((bf16[128,256]{0,1:T(8,128)(2,1)S(1)}, bf16[128,256]{0,1:T(8,128)(2,1)S(1)}, u32[]{:S(2)}, u32[]{:S(2)}) %collective-permute-start.5) | collective-permute-done | bytes 65568 | tf_op jit(solution)/shard_map/ppermute | solution.py:13
  159.1 3.7 scatter_fusion
  169.3 3.3 collective-permute-start.10
  172.5 3.4 collective-permute-start.9
  175.9 7.6 %collective-permute-done.9 = bf16[128,256]{1,0:T(8,128)(2,1)S(1)} collective-permute-done((bf16[128,256]{1,0:T(8,128)(2,1)S(1)}, bf16[128,256]{1,0:T(8,128)(2,1)S(1)}, u32[]{:S(2)}, u32[]{:S(2)}) %collective-permute-start.9) | collective-permute-done | bytes 65568 | tf_op jit(solution)/shard_map/ppermute | solution.py:13
  183.5 3.8 fusion.54
  191.2 3.6 collective-permute-start.14
  194.9 3.4 collective-permute-start.13
  200.9 3.4 collective-permute-done.13
  206.5 3.9 scatter_fusion.1
  218.6 3.6 collective-permute-start.18
  222.3 3.1 collective-permute-start.17
  225.4 6.8 %collective-permute-done.17 = bf16[128,256]{1,0:T(8,128)(2,1)S(1)} collective-permute-done((bf16[128,256]{1,0:T(8,128)(2,1)S(1)}, bf16[128,256]{1,0:T(8,128)(2,1)S(1)}, u32[]{:S(2)}, u32[]{:S(2)}) %collective-permute-start.17) | collective-permute-done | bytes 65568 | tf_op jit(solution)/shard_map/ppermute | solution.py:13
  232.5 18.0 %all_gather.10 = bf16[512,256]{1,0:T(8,128)(2,1)S(1)} all-gather(bf16[32,256]{1,0:T(8,128)(2,1)S(1)} %fusion.23), channel_id=1, replica_groups=mesh['row'=16,'col'=16] {'col'}, dimensions={0}, use_global_device_ids=true | all-gather | bytes 278528 | tf_op jit(solution)/shard_map/all_gather | solution.py:75
  251.7 5.0 fusion.6
  256.7 77.3 %reduce-scatter.12.cloned.1.call-done = bf16[32,256]{1,0:T(8,128)(2,1)} async-done(((bf16[512,256]{1,0:T(8,128)(2,1)}), bf16[32,256]{1,0:T(8,128)(2,1)}) %reduce-scatter.12.cloned.1.call-update) | async-done | bytes 16400
  335.8 4.5 collective-permute-start.20
  340.3 5.0 collective-permute-start.23
  345.3 3.0 collective-permute-start.22
  352.9 6.8 %collective-permute-done.21 = bf16[128,256]{0,1:T(8,128)(2,1)S(1)} collective-permute-done((bf16[128,256]{0,1:T(8,128)(2,1)S(1)}, bf16[128,256]{0,1:T(8,128)(2,1)S(1)}, u32[]{:S(2)}, u32[]{:S(2)}) %collective-permute-start.21) | collective-permute-done | bytes 65568 | tf_op jit(solution)/shard_map/ppermute | solution.py:13
  361.9 3.7 scatter_fusion.2
  372.2 3.3 collective-permute-start.26
  375.4 3.4 collective-permute-start.25
  378.8 7.6 %collective-permute-done.25 = bf16[128,256]{1,0:T(8,128)(2,1)S(1)} collective-permute-done((bf16[128,256]{1,0:T(8,128)(2,1)S(1)}, bf16[128,256]{1,0:T(8,128)(2,1)S(1)}, u32[]{:S(2)}, u32[]{:S(2)}) %collective-permute-start.25) | collective-permute-done | bytes 65568 | tf_op jit(solution)/shard_map/ppermute | solution.py:13
  386.4 3.8 fusion.56
  394.3 3.6 collective-permute-start.30
  398.0 3.4 collective-permute-start.29
  409.6 5.2 scatter_fusion.3
  418.6 3.8 collective-permute-start.32
  424.3 3.6 collective-permute-start.34
  429.9 8.0 %collective-permute-done.33 = bf16[128,256]{1,0:T(8,128)(2,1)S(1)} collective-permute-done((bf16[128,256]{1,0:T(8,128)(2,1)S(1)}, bf16[128,256]{1,0:T(8,128)(2,1)S(1)}, u32[]{:S(2)}, u32[]{:S(2)}) %collective-permute-start.33) | collective-permute-done | bytes 65568 | tf_op jit(solution)/shard_map/ppermute | solution.py:13
  438.6 17.8 %all_gather.11 = bf16[512,256]{1,0:T(8,128)(2,1)S(1)} all-gather(bf16[32,256]{1,0:T(8,128)(2,1)S(1)} %fusion.24), channel_id=1, replica_groups=mesh['row'=16,'col'=16] {'col'}, dimensions={0}, use_global_device_ids=true | all-gather | bytes 278528 | tf_op jit(solution)/shard_map/all_gather | solution.py:75
  457.7 5.0 fusion.4
  462.7 77.3 %reduce-scatter.14.cloned.1.call-done = bf16[32,256]{1,0:T(8,128)(2,1)} async-done(((bf16[512,256]{1,0:T(8,128)(2,1)}), bf16[32,256]{1,0:T(8,128)(2,1)}) %reduce-scatter.14.cloned.1.call-update) | async-done | bytes 16400
  541.9 4.5 collective-permute-start.36
  546.4 5.0 collective-permute-start.39
  551.4 3.0 collective-permute-start.38
  560.0 5.7 collective-permute-done.37
  567.8 5.2 scatter_fusion.4
  (131 shorter events, 88.9 us)
Async XLA Ops:
  6.5 46.5 %copy-start = (bf16[16,32,512]{2,1,0:T(8,128)(2,1)S(1)}, bf16[16,32,512]{2,1,0:T(8,128)(2,1)}, u32[]{:S(2)}) copy-start(bf16[16,32,512]{2,1,0:T(8,128)(2,1)} %param.11) | copy-start | bytes 1572868
  6.5 127.1 %reduce-scatter.10.cloned.1.call-start = ((), (), s32[]{:S(2)}) async-start(), calls=%async_computation.3 | async-start | bytes 278528
  9.3 24.4 %copy-start.1 = (bf16[1,1,1536,32]{2,3,1,0:T(8,128)(2,1)S(1)}, bf16[1,1,1536,32]{2,3,1,0:T(8,128)(2,1)}, u32[]{:S(2)}) copy-start(bf16[1,1,1536,32]{2,3,1,0:T(8,128)(2,1)} %param.10) | copy-start | bytes 294916
  11.4 13.6 %collective-permute-start = (bf16[128,256]{1,0:T(8,128)(2,1)S(1)}, bf16[128,256]{1,0:T(8,128)(2,1)S(1)}, u32[]{:S(2)}, u32[]{:S(2)}) collective-permute-start(bf16[128,256]{1,0:T(8,128)(2,1)S(1)} %get-tuple-element.41), channel_id=1, source_target_pairs={{0,16},{16,32},{32,48},{48,64},{64,80},{80,96},{96,112},{112,128},... | collective-permute-start | bytes 196616 | tf_op jit(solution)/shard_map/ppermute | solution.py:13
  17.2 7.8 %collective-permute-start.3 = (bf16[128,256]{1,0:T(8,128)(2,1)S(1)}, bf16[128,256]{1,0:T(8,128)(2,1)S(1)}, u32[]{:S(2)}, u32[]{:S(2)}) collective-permute-start(bf16[128,256]{1,0:T(8,128)(2,1)S(1)} %get-tuple-element.42), channel_id=1, source_target_pairs={{1,0},{2,1},{3,2},{4,3},{5,4},{6,5},{7,6},{8,7},{9,8},{10,9},{11,1... | collective-permute-start | bytes 196616 | tf_op jit(solution)/shard_map/ppermute | solution.py:13
  20.1 5.0 collective-permute-start.2
  23.1 10.5 %collective-permute-start.1 = (bf16[128,256]{1,0:T(8,128)(2,1)S(1)}, bf16[128,256]{1,0:T(8,128)(2,1)S(1)}, u32[]{:S(2)}, u32[]{:S(2)}) collective-permute-start(bf16[128,256]{1,0:T(8,128)(2,1)S(1)} %get-tuple-element.44), channel_id=1, source_target_pairs={{16,0},{32,16},{48,32},{64,48},{80,64},{96,80},{112,96},{128,112},... | collective-permute-start | bytes 196616 | tf_op jit(solution)/shard_map/ppermute | solution.py:13
  54.2 279.7 %reduce-scatter.12.cloned.1.call-start = ((), (), s32[]{:S(2)}) async-start(), calls=%async_computation.4 | async-start | bytes 278528
  134.8 14.8 %collective-permute-start.4 = (bf16[128,256]{0,1:T(8,128)(2,1)S(1)}, bf16[128,256]{0,1:T(8,128)(2,1)S(1)}, u32[]{:S(2)}, u32[]{:S(2)}) collective-permute-start(bf16[128,256]{0,1:T(8,128)(2,1)S(1)} %get-tuple-element.21), channel_id=1, source_target_pairs={{0,16},{16,32},{32,48},{48,64},{64,80},{80,96},{96,112},{112,128},... | collective-permute-start | bytes 196616 | tf_op jit(solution)/shard_map/ppermute | solution.py:13
  139.3 10.4 %collective-permute-start.7 = (bf16[128,256]{0,1:T(8,128)(2,1)S(1)}, bf16[128,256]{0,1:T(8,128)(2,1)S(1)}, u32[]{:S(2)}, u32[]{:S(2)}) collective-permute-start(bf16[128,256]{0,1:T(8,128)(2,1)S(1)} %get-tuple-element.22), channel_id=1, source_target_pairs={{1,0},{2,1},{3,2},{4,3},{5,4},{6,5},{7,6},{8,7},{9,8},{10,9},{11,1... | collective-permute-start | bytes 196616 | tf_op jit(solution)/shard_map/ppermute | solution.py:13
  144.3 5.4 collective-permute-start.6
  147.3 11.4 %collective-permute-start.5 = (bf16[128,256]{0,1:T(8,128)(2,1)S(1)}, bf16[128,256]{0,1:T(8,128)(2,1)S(1)}, u32[]{:S(2)}, u32[]{:S(2)}) collective-permute-start(bf16[128,256]{0,1:T(8,128)(2,1)S(1)} %get-tuple-element.24), channel_id=1, source_target_pairs={{16,0},{32,16},{48,32},{64,48},{80,64},{96,80},{112,96},{128,112},... | collective-permute-start | bytes 196616 | tf_op jit(solution)/shard_map/ppermute | solution.py:13
  165.0 10.9 %collective-permute-start.8 = (bf16[128,256]{1,0:T(8,128)(2,1)S(1)}, bf16[128,256]{1,0:T(8,128)(2,1)S(1)}, u32[]{:S(2)}, u32[]{:S(2)}) collective-permute-start(bf16[128,256]{1,0:T(8,128)(2,1)S(1)} %get-tuple-element.37), channel_id=1, source_target_pairs={{0,16},{16,32},{32,48},{48,64},{64,80},{80,96},{96,112},{112,128},... | collective-permute-start | bytes 196616 | tf_op jit(solution)/shard_map/ppermute | solution.py:13
  166.9 9.0 %collective-permute-start.11 = (bf16[128,256]{1,0:T(8,128)(2,1)S(1)}, bf16[128,256]{1,0:T(8,128)(2,1)S(1)}, u32[]{:S(2)}, u32[]{:S(2)}) collective-permute-start(bf16[128,256]{1,0:T(8,128)(2,1)S(1)} %get-tuple-element.38), channel_id=1, source_target_pairs={{1,0},{2,1},{3,2},{4,3},{5,4},{6,5},{7,6},{8,7},{9,8},{10,9},{11,1... | collective-permute-start | bytes 196616 | tf_op jit(solution)/shard_map/ppermute | solution.py:13
  169.3 6.7 %collective-permute-start.10 = (bf16[128,256]{1,0:T(8,128)(2,1)S(1)}, bf16[128,256]{1,0:T(8,128)(2,1)S(1)}, u32[]{:S(2)}, u32[]{:S(2)}) collective-permute-start(bf16[128,256]{1,0:T(8,128)(2,1)S(1)} %get-tuple-element.39), channel_id=1, source_target_pairs={{0,1},{1,2},{2,3},{3,4},{4,5},{5,6},{6,7},{7,8},{8,9},{9,10},{10,1... | collective-permute-start | bytes 196616 | tf_op jit(solution)/shard_map/ppermute | solution.py:13
  172.5 11.0 %collective-permute-start.9 = (bf16[128,256]{1,0:T(8,128)(2,1)S(1)}, bf16[128,256]{1,0:T(8,128)(2,1)S(1)}, u32[]{:S(2)}, u32[]{:S(2)}) collective-permute-start(bf16[128,256]{1,0:T(8,128)(2,1)S(1)} %get-tuple-element.40), channel_id=1, source_target_pairs={{16,0},{32,16},{48,32},{64,48},{80,64},{96,80},{112,96},{128,112},... | collective-permute-start | bytes 196616 | tf_op jit(solution)/shard_map/ppermute | solution.py:13
  187.4 13.5 %collective-permute-start.12 = (bf16[128,256]{0,1:T(8,128)(2,1)S(1)}, bf16[128,256]{0,1:T(8,128)(2,1)S(1)}, u32[]{:S(2)}, u32[]{:S(2)}) collective-permute-start(bf16[128,256]{0,1:T(8,128)(2,1)S(1)} %get-tuple-element.17), channel_id=1, source_target_pairs={{0,16},{16,32},{32,48},{48,64},{64,80},{80,96},{96,112},{112,128},... | collective-permute-start | bytes 196616 | tf_op jit(solution)/shard_map/ppermute | solution.py:13
  189.3 11.6 %collective-permute-start.15 = (bf16[128,256]{0,1:T(8,128)(2,1)S(1)}, bf16[128,256]{0,1:T(8,128)(2,1)S(1)}, u32[]{:S(2)}, u32[]{:S(2)}) collective-permute-start(bf16[128,256]{0,1:T(8,128)(2,1)S(1)} %get-tuple-element.18), channel_id=1, source_target_pairs={{1,0},{2,1},{3,2},{4,3},{5,4},{6,5},{7,6},{8,7},{9,8},{10,9},{11,1... | collective-permute-start | bytes 196616 | tf_op jit(solution)/shard_map/ppermute | solution.py:13
  191.2 9.7 %collective-permute-start.14 = (bf16[128,256]{0,1:T(8,128)(2,1)S(1)}, bf16[128,256]{0,1:T(8,128)(2,1)S(1)}, u32[]{:S(2)}, u32[]{:S(2)}) collective-permute-start(bf16[128,256]{0,1:T(8,128)(2,1)S(1)} %get-tuple-element.19), channel_id=1, source_target_pairs={{0,1},{1,2},{2,3},{3,4},{4,5},{5,6},{6,7},{7,8},{8,9},{9,10},{10,1... | collective-permute-start | bytes 196616 | tf_op jit(solution)/shard_map/ppermute | solution.py:13
  194.9 9.4 %collective-permute-start.13 = (bf16[128,256]{0,1:T(8,128)(2,1)S(1)}, bf16[128,256]{0,1:T(8,128)(2,1)S(1)}, u32[]{:S(2)}, u32[]{:S(2)}) collective-permute-start(bf16[128,256]{0,1:T(8,128)(2,1)S(1)} %get-tuple-element.20), channel_id=1, source_target_pairs={{16,0},{32,16},{48,32},{64,48},{80,64},{96,80},{112,96},{128,112},... | collective-permute-start | bytes 196616 | tf_op jit(solution)/shard_map/ppermute | solution.py:13
  213.9 11.4 %collective-permute-start.16 = (bf16[128,256]{1,0:T(8,128)(2,1)S(1)}, bf16[128,256]{1,0:T(8,128)(2,1)S(1)}, u32[]{:S(2)}, u32[]{:S(2)}) collective-permute-start(bf16[128,256]{1,0:T(8,128)(2,1)S(1)} %get-tuple-element.33), channel_id=1, source_target_pairs={{0,16},{16,32},{32,48},{48,64},{64,80},{80,96},{96,112},{112,128},... | collective-permute-start | bytes 196616 | tf_op jit(solution)/shard_map/ppermute | solution.py:13
  216.7 8.7 %collective-permute-start.19 = (bf16[128,256]{1,0:T(8,128)(2,1)S(1)}, bf16[128,256]{1,0:T(8,128)(2,1)S(1)}, u32[]{:S(2)}, u32[]{:S(2)}) collective-permute-start(bf16[128,256]{1,0:T(8,128)(2,1)S(1)} %get-tuple-element.34), channel_id=1, source_target_pairs={{1,0},{2,1},{3,2},{4,3},{5,4},{6,5},{7,6},{8,7},{9,8},{10,9},{11,1... | collective-permute-start | bytes 196616 | tf_op jit(solution)/shard_map/ppermute | solution.py:13
  218.6 6.7 %collective-permute-start.18 = (bf16[128,256]{1,0:T(8,128)(2,1)S(1)}, bf16[128,256]{1,0:T(8,128)(2,1)S(1)}, u32[]{:S(2)}, u32[]{:S(2)}) collective-permute-start(bf16[128,256]{1,0:T(8,128)(2,1)S(1)} %get-tuple-element.35), channel_id=1, source_target_pairs={{0,1},{1,2},{2,3},{3,4},{4,5},{5,6},{6,7},{7,8},{8,9},{9,10},{10,1... | collective-permute-start | bytes 196616 | tf_op jit(solution)/shard_map/ppermute | solution.py:13
  222.3 9.9 %collective-permute-start.17 = (bf16[128,256]{1,0:T(8,128)(2,1)S(1)}, bf16[128,256]{1,0:T(8,128)(2,1)S(1)}, u32[]{:S(2)}, u32[]{:S(2)}) collective-permute-start(bf16[128,256]{1,0:T(8,128)(2,1)S(1)} %get-tuple-element.36), channel_id=1, source_target_pairs={{16,0},{32,16},{48,32},{64,48},{80,64},{96,80},{112,96},{128,112},... | collective-permute-start | bytes 196616 | tf_op jit(solution)/shard_map/ppermute | solution.py:13
  251.7 288.4 %reduce-scatter.14.cloned.1.call-start = ((), (), s32[]{:S(2)}) async-start(), calls=%async_computation.5 | async-start | bytes 278528
  335.8 17.1 %collective-permute-start.20 = (bf16[128,256]{0,1:T(8,128)(2,1)S(1)}, bf16[128,256]{0,1:T(8,128)(2,1)S(1)}, u32[]{:S(2)}, u32[]{:S(2)}) collective-permute-start(bf16[128,256]{0,1:T(8,128)(2,1)S(1)} %get-tuple-element.13), channel_id=1, source_target_pairs={{0,16},{16,32},{32,48},{48,64},{64,80},{80,96},{96,112},{112,128},... | collective-permute-start | bytes 196616 | tf_op jit(solution)/shard_map/ppermute | solution.py:13
  340.3 12.6 %collective-permute-start.23 = (bf16[128,256]{0,1:T(8,128)(2,1)S(1)}, bf16[128,256]{0,1:T(8,128)(2,1)S(1)}, u32[]{:S(2)}, u32[]{:S(2)}) collective-permute-start(bf16[128,256]{0,1:T(8,128)(2,1)S(1)} %get-tuple-element.14), channel_id=1, source_target_pairs={{1,0},{2,1},{3,2},{4,3},{5,4},{6,5},{7,6},{8,7},{9,8},{10,9},{11,1... | collective-permute-start | bytes 196616 | tf_op jit(solution)/shard_map/ppermute | solution.py:13
  345.3 7.6 %collective-permute-start.22 = (bf16[128,256]{0,1:T(8,128)(2,1)S(1)}, bf16[128,256]{0,1:T(8,128)(2,1)S(1)}, u32[]{:S(2)}, u32[]{:S(2)}) collective-permute-start(bf16[128,256]{0,1:T(8,128)(2,1)S(1)} %get-tuple-element.15), channel_id=1, source_target_pairs={{0,1},{1,2},{2,3},{3,4},{4,5},{5,6},{6,7},{7,8},{8,9},{9,10},{10,1... | collective-permute-start | bytes 196616 | tf_op jit(solution)/shard_map/ppermute | solution.py:13
  348.3 11.4 %collective-permute-start.21 = (bf16[128,256]{0,1:T(8,128)(2,1)S(1)}, bf16[128,256]{0,1:T(8,128)(2,1)S(1)}, u32[]{:S(2)}, u32[]{:S(2)}) collective-permute-start(bf16[128,256]{0,1:T(8,128)(2,1)S(1)} %get-tuple-element.16), channel_id=1, source_target_pairs={{16,0},{32,16},{48,32},{64,48},{80,64},{96,80},{112,96},{128,112},... | collective-permute-start | bytes 196616 | tf_op jit(solution)/shard_map/ppermute | solution.py:13
  367.9 10.9 %collective-permute-start.24 = (bf16[128,256]{1,0:T(8,128)(2,1)S(1)}, bf16[128,256]{1,0:T(8,128)(2,1)S(1)}, u32[]{:S(2)}, u32[]{:S(2)}) collective-permute-start(bf16[128,256]{1,0:T(8,128)(2,1)S(1)} %get-tuple-element.29), channel_id=1, source_target_pairs={{0,16},{16,32},{32,48},{48,64},{64,80},{80,96},{96,112},{112,128},... | collective-permute-start | bytes 196616 | tf_op jit(solution)/shard_map/ppermute | solution.py:13
  369.8 9.0 %collective-permute-start.27 = (bf16[128,256]{1,0:T(8,128)(2,1)S(1)}, bf16[128,256]{1,0:T(8,128)(2,1)S(1)}, u32[]{:S(2)}, u32[]{:S(2)}) collective-permute-start(bf16[128,256]{1,0:T(8,128)(2,1)S(1)} %get-tuple-element.30), channel_id=1, source_target_pairs={{1,0},{2,1},{3,2},{4,3},{5,4},{6,5},{7,6},{8,7},{9,8},{10,9},{11,1... | collective-permute-start | bytes 196616 | tf_op jit(solution)/shard_map/ppermute | solution.py:13
  372.2 6.7 %collective-permute-start.26 = (bf16[128,256]{1,0:T(8,128)(2,1)S(1)}, bf16[128,256]{1,0:T(8,128)(2,1)S(1)}, u32[]{:S(2)}, u32[]{:S(2)}) collective-permute-start(bf16[128,256]{1,0:T(8,128)(2,1)S(1)} %get-tuple-element.31), channel_id=1, source_target_pairs={{0,1},{1,2},{2,3},{3,4},{4,5},{5,6},{6,7},{7,8},{8,9},{9,10},{10,1... | collective-permute-start | bytes 196616 | tf_op jit(solution)/shard_map/ppermute | solution.py:13
  375.4 11.0 %collective-permute-start.25 = (bf16[128,256]{1,0:T(8,128)(2,1)S(1)}, bf16[128,256]{1,0:T(8,128)(2,1)S(1)}, u32[]{:S(2)}, u32[]{:S(2)}) collective-permute-start(bf16[128,256]{1,0:T(8,128)(2,1)S(1)} %get-tuple-element.32), channel_id=1, source_target_pairs={{16,0},{32,16},{48,32},{64,48},{80,64},{96,80},{112,96},{128,112},... | collective-permute-start | bytes 196616 | tf_op jit(solution)/shard_map/ppermute | solution.py:13
  390.3 14.7 %collective-permute-start.28 = (bf16[128,256]{0,1:T(8,128)(2,1)S(1)}, bf16[128,256]{0,1:T(8,128)(2,1)S(1)}, u32[]{:S(2)}, u32[]{:S(2)}) collective-permute-start(bf16[128,256]{0,1:T(8,128)(2,1)S(1)} %get-tuple-element.9), channel_id=1, source_target_pairs={{0,16},{16,32},{32,48},{48,64},{64,80},{80,96},{96,112},{112,128},... | collective-permute-start | bytes 196616 | tf_op jit(solution)/shard_map/ppermute | solution.py:13
  392.4 12.6 %collective-permute-start.31 = (bf16[128,256]{0,1:T(8,128)(2,1)S(1)}, bf16[128,256]{0,1:T(8,128)(2,1)S(1)}, u32[]{:S(2)}, u32[]{:S(2)}) collective-permute-start(bf16[128,256]{0,1:T(8,128)(2,1)S(1)} %get-tuple-element.10), channel_id=1, source_target_pairs={{1,0},{2,1},{3,2},{4,3},{5,4},{6,5},{7,6},{8,7},{9,8},{10,9},{11,1... | collective-permute-start | bytes 196616 | tf_op jit(solution)/shard_map/ppermute | solution.py:13
  394.3 10.6 %collective-permute-start.30 = (bf16[128,256]{0,1:T(8,128)(2,1)S(1)}, bf16[128,256]{0,1:T(8,128)(2,1)S(1)}, u32[]{:S(2)}, u32[]{:S(2)}) collective-permute-start(bf16[128,256]{0,1:T(8,128)(2,1)S(1)} %get-tuple-element.11), channel_id=1, source_target_pairs={{0,1},{1,2},{2,3},{3,4},{4,5},{5,6},{6,7},{7,8},{8,9},{9,10},{10,1... | collective-permute-start | bytes 196616 | tf_op jit(solution)/shard_map/ppermute | solution.py:13
  398.0 9.4 %collective-permute-start.29 = (bf16[128,256]{0,1:T(8,128)(2,1)S(1)}, bf16[128,256]{0,1:T(8,128)(2,1)S(1)}, u32[]{:S(2)}, u32[]{:S(2)}) collective-permute-start(bf16[128,256]{0,1:T(8,128)(2,1)S(1)} %get-tuple-element.12), channel_id=1, source_target_pairs={{16,0},{32,16},{48,32},{64,48},{80,64},{96,80},{112,96},{128,112},... | collective-permute-start | bytes 196616 | tf_op jit(solution)/shard_map/ppermute | solution.py:13
  418.6 11.3 %collective-permute-start.32 = (bf16[128,256]{1,0:T(8,128)(2,1)S(1)}, bf16[128,256]{1,0:T(8,128)(2,1)S(1)}, u32[]{:S(2)}, u32[]{:S(2)}) collective-permute-start(bf16[128,256]{1,0:T(8,128)(2,1)S(1)} %get-tuple-element.25), channel_id=1, source_target_pairs={{0,16},{16,32},{32,48},{48,64},{64,80},{80,96},{96,112},{112,128},... | collective-permute-start | bytes 196616 | tf_op jit(solution)/shard_map/ppermute | solution.py:13
  422.4 7.5 %collective-permute-start.35 = (bf16[128,256]{1,0:T(8,128)(2,1)S(1)}, bf16[128,256]{1,0:T(8,128)(2,1)S(1)}, u32[]{:S(2)}, u32[]{:S(2)}) collective-permute-start(bf16[128,256]{1,0:T(8,128)(2,1)S(1)} %get-tuple-element.26), channel_id=1, source_target_pairs={{1,0},{2,1},{3,2},{4,3},{5,4},{6,5},{7,6},{8,7},{9,8},{10,9},{11,1... | collective-permute-start | bytes 196616 | tf_op jit(solution)/shard_map/ppermute | solution.py:13
  424.3 5.6 collective-permute-start.34
  428.0 9.9 %collective-permute-start.33 = (bf16[128,256]{1,0:T(8,128)(2,1)S(1)}, bf16[128,256]{1,0:T(8,128)(2,1)S(1)}, u32[]{:S(2)}, u32[]{:S(2)}) collective-permute-start(bf16[128,256]{1,0:T(8,128)(2,1)S(1)} %get-tuple-element.28), channel_id=1, source_target_pairs={{16,0},{32,16},{48,32},{64,48},{80,64},{96,80},{112,96},{128,112},... | collective-permute-start | bytes 196616 | tf_op jit(solution)/shard_map/ppermute | solution.py:13
  437.9 0.7 copy-start.2
  541.9 18.0 %collective-permute-start.36 = (bf16[128,256]{0,1:T(8,128)(2,1)S(1)}, bf16[128,256]{0,1:T(8,128)(2,1)S(1)}, u32[]{:S(2)}, u32[]{:S(2)}) collective-permute-start(bf16[128,256]{0,1:T(8,128)(2,1)S(1)} %get-tuple-element.5), channel_id=1, source_target_pairs={{0,16},{16,32},{32,48},{48,64},{64,80},{80,96},{96,112},{112,128},... | collective-permute-start | bytes 196616 | tf_op jit(solution)/shard_map/ppermute | solution.py:13
  546.4 13.5 %collective-permute-start.39 = (bf16[128,256]{0,1:T(8,128)(2,1)S(1)}, bf16[128,256]{0,1:T(8,128)(2,1)S(1)}, u32[]{:S(2)}, u32[]{:S(2)}) collective-permute-start(bf16[128,256]{0,1:T(8,128)(2,1)S(1)} %get-tuple-element.6), channel_id=1, source_target_pairs={{1,0},{2,1},{3,2},{4,3},{5,4},{6,5},{7,6},{8,7},{9,8},{10,9},{11,1... | collective-permute-start | bytes 196616 | tf_op jit(solution)/shard_map/ppermute | solution.py:13
  551.4 8.6 %collective-permute-start.38 = (bf16[128,256]{0,1:T(8,128)(2,1)S(1)}, bf16[128,256]{0,1:T(8,128)(2,1)S(1)}, u32[]{:S(2)}, u32[]{:S(2)}) collective-permute-start(bf16[128,256]{0,1:T(8,128)(2,1)S(1)} %get-tuple-element.7), channel_id=1, source_target_pairs={{0,1},{1,2},{2,3},{3,4},{4,5},{5,6},{6,7},{7,8},{8,9},{9,10},{10,1... | collective-permute-start | bytes 196616 | tf_op jit(solution)/shard_map/ppermute | solution.py:13
  554.4 11.2 %collective-permute-start.37 = (bf16[128,256]{0,1:T(8,128)(2,1)S(1)}, bf16[128,256]{0,1:T(8,128)(2,1)S(1)}, u32[]{:S(2)}, u32[]{:S(2)}) collective-permute-start(bf16[128,256]{0,1:T(8,128)(2,1)S(1)} %get-tuple-element.8), channel_id=1, source_target_pairs={{16,0},{32,16},{48,32},{64,48},{80,64},{96,80},{112,96},{128,112},... | collective-permute-start | bytes 196616 | tf_op jit(solution)/shard_map/ppermute | solution.py:13
Sparse Core Ops, SparseCore 0:
  54.3 79.2 reduce-scatter.9
  251.8 82.0 reduce-scatter.11
  457.8 82.2 reduce-scatter.13
where the time goes:
time: 584 us; the launch traced here: 582 us
  waiting for transfers between devices  296 us (51%)
  starting transfers between devices  123 us (21%)
  blocking collectives  54.9 us (9%)
  other arithmetic  36 us (6%)
  local copies, waits for them, and re-layouts  30.1 us (5%)
  matrix products  27.8 us (5%)
  between operations  14.1 us (2%)
    unnamed x6, waiting for transfers between devices  230 us
    ppermute x40, starting transfers between devices, passed_along(): return lax.ppermute(shard, axis, pairs)  123 us
    ppermute x40, waiting for transfers between devices, passed_along(): return lax.ppermute(shard, axis, pairs)  65.8 us
    all_gather x3, blocking collectives, per_device(): block_rows = lax.all_gather(restricted, 'col', axis=0, tiled=True)  54.9 us
    scatter-add x5, other arithmetic, owner_sum(): summed = jnp.zeros((own_rows, columns), jnp.float32).at[flat_rows].add(we...  21.8 us
    dot_general x3, matrix products, per_device(): jnp.dot(inverse, residual_local, preferred_element_type=jnp.float32)  13.8 us
    slice x10, local copies, waits for them, and re-layouts, owner_sum(): return local_terms[:own_rows] + summed  12.9 us
  transfers between devices with their start and end apart: 43, of which 13 were waited for; matrix products, arithmetic and copies ran while one was open for 5% of the time, Pallas kernels for 0%

commit v1 on v0

--- a/solution.py
+++ b/solution.py
@@ -72,7 +72,15 @@
             prolong, residual_local, (((0,), (0,)), ((), ())), preferred_element_type=jnp.float32
         )
         restricted = restricted.astype(jnp.bfloat16)
-        block_rows = lax.all_gather(restricted, "col", axis=0, tiled=True)
+
+        def mark_the_yards(t0):
+            u_next = lax.psum(1, axis_name="col")
+            shaped = jnp.stack(u_next * [t0])
+            a_now = lax.all_to_all(shaped, axis_name="col", split_axis=0, concat_axis=0)
+            then = jnp.concatenate(a_now, axis=0)
+            return then
+
+        block_rows = mark_the_yards(restricted)
         solved = lax.psum_scatter(
             jnp.dot(coarse_rows, block_rows, preferred_element_type=jnp.float32).astype(
                 jnp.bfloat16

time: 584 us -> 564 us (0.966)
  blocking collectives: 54.9 us -> 40.8 us
  waiting for transfers between devices: 296 us -> 290 us
    all_gather x3 -> x0, blocking collectives: 54.9 us -> none  [per_device(): block_rows = lax.all_gather(restricted, 'col', axis=0, tiled=True)]
    all_to_all x0 -> x3, blocking collectives: none -> 40.8 us  [mark_the_yards(): a_now = lax.all_to_all(shaped, axis_name='col', split_axis=0, concat_axis=0)]
where the time goes in v1:
time: 564 us; the launch traced here: 562 us
  waiting for transfers between devices  290 us (51%)
  starting transfers between devices  123 us (22%)
  blocking collectives  40.8 us (7%)
  other arithmetic  36 us (6%)
  local copies, waits for them, and re-layouts  29.8 us (5%)
  matrix products  27.8 us (5%)
  between operations  14.1 us (2%)
    unnamed x6, waiting for transfers between devices  225 us
    ppermute x40, starting transfers between devices, passed_along(): return lax.ppermute(shard, axis, pairs)  123 us
    ppermute x40, waiting for transfers between devices, passed_along(): return lax.ppermute(shard, axis, pairs)  65 us
    all_to_all x3, blocking collectives, mark_the_yards(): a_now = lax.all_to_all(shaped, axis_name='col', split_axis=0, concat_axis=0)  40.8 us
    scatter-add x5, other arithmetic, owner_sum(): summed = jnp.zeros((own_rows, columns), jnp.float32).at[flat_rows].add(we...  21.8 us
    dot_general x3, matrix products, per_device(): jnp.dot(inverse, residual_local, preferred_element_type=jnp.float32)  13.8 us
    slice x10, local copies, waits for them, and re-layouts, owner_sum(): return local_terms[:own_rows] + summed  12.9 us
  transfers between devices with their start and end apart: 43, of which 13 were waited for; matrix products, arithmetic and copies ran while one was open for 5% of the time, Pallas kernels for 0%

profile of v1, /device:TPU:89, one launch (start us, length us, event | category | flops | bytes accessed | tf_op | source)
XLA Modules:
  0.0 562.3 jit_solution(9247706597383473492)
XLA Ops:
  11.4 5.8 %collective-permute-start = (bf16[128,256]{1,0:T(8,128)(2,1)S(1)}, bf16[128,256]{1,0:T(8,128)(2,1)S(1)}, u32[]{:S(2)}, u32[]{:S(2)}) collective-permute-start(bf16[128,256]{1,0:T(8,128)(2,1)S(1)} %get-tuple-element.41), channel_id=1, source_target_pairs={{0,16},{16,32},{32,48},{48,64},{64,80},{80,96},{96,112},{112,128},... | collective-permute-start | bytes 196616 | tf_op jit(solution)/shard_map/ppermute | solution.py:13
  20.1 3.0 collective-permute-start.2
  25.1 8.6 %collective-permute-done.1 = bf16[128,256]{1,0:T(8,128)(2,1)S(1)} collective-permute-done((bf16[128,256]{1,0:T(8,128)(2,1)S(1)}, bf16[128,256]{1,0:T(8,128)(2,1)S(1)}, u32[]{:S(2)}, u32[]{:S(2)}) %collective-permute-start.1) | collective-permute-done | bytes 65568 | tf_op jit(solution)/shard_map/ppermute | solution.py:13
  34.0 12.5 %all_to_all.15 = bf16[16,32,256]{2,1,0:T(8,128)(2,1)S(1)} all-to-all(bf16[16,32,256]{2,1,0:T(8,128)(2,1)S(1)} %stack.212), channel_id=1, replica_groups=mesh['row'=16,'col'=16] {'col'}, dimensions={0} | all-to-all | bytes 524288 | tf_op jit(solution)/shard_map/all_to_all | solution.py:79
  47.7 3.8 fusion.8
  51.5 75.9 %reduce-scatter.10.cloned.1.call-done = bf16[32,256]{1,0:T(8,128)(2,1)} async-done(((bf16[512,256]{1,0:T(8,128)(2,1)}), bf16[32,256]{1,0:T(8,128)(2,1)}) %reduce-scatter.10.cloned.1.call-update) | async-done | bytes 16400
  128.6 4.3 collective-permute-start.4
  132.9 5.2 collective-permute-start.7
  138.1 3.0 collective-permute-start.6
  143.5 8.8 %collective-permute-done.5 = bf16[128,256]{0,1:T(8,128)(2,1)S(1)} collective-permute-done((bf16[128,256]{0,1:T(8,128)(2,1)S(1)}, bf16[128,256]{0,1:T(8,128)(2,1)S(1)}, u32[]{:S(2)}, u32[]{:S(2)}) %collective-permute-start.5) | collective-permute-done | bytes 65568 | tf_op jit(solution)/shard_map/ppermute | solution.py:13
  152.7 3.7 scatter_fusion
  162.5 3.6 collective-permute-start.10
  166.2 3.4 collective-permute-start.9
  169.6 7.2 %collective-permute-done.9 = bf16[128,256]{1,0:T(8,128)(2,1)S(1)} collective-permute-done((bf16[128,256]{1,0:T(8,128)(2,1)S(1)}, bf16[128,256]{1,0:T(8,128)(2,1)S(1)}, u32[]{:S(2)}, u32[]{:S(2)}) %collective-permute-start.9) | collective-permute-done | bytes 65568 | tf_op jit(solution)/shard_map/ppermute | solution.py:13
  176.8 3.8 fusion.54
  184.5 3.6 collective-permute-start.14
  188.2 3.4 collective-permute-start.13
  194.2 3.5 collective-permute-done.13
  200.0 3.9 scatter_fusion.1
  211.9 3.6 collective-permute-start.18
  215.6 3.5 collective-permute-start.17
  219.1 6.4 %collective-permute-done.17 = bf16[128,256]{1,0:T(8,128)(2,1)S(1)} collective-permute-done((bf16[128,256]{1,0:T(8,128)(2,1)S(1)}, bf16[128,256]{1,0:T(8,128)(2,1)S(1)}, u32[]{:S(2)}, u32[]{:S(2)}) %collective-permute-start.17) | collective-permute-done | bytes 65568 | tf_op jit(solution)/shard_map/ppermute | solution.py:13
  225.8 14.0 %all_to_all.16 = bf16[16,32,256]{2,1,0:T(8,128)(2,1)S(1)} all-to-all(bf16[16,32,256]{2,1,0:T(8,128)(2,1)S(1)} %stack.233), channel_id=1, replica_groups=mesh['row'=16,'col'=16] {'col'}, dimensions={0} | all-to-all | bytes 524288 | tf_op jit(solution)/shard_map/all_to_all | solution.py:79
  241.1 5.0 fusion.6
  246.0 74.8 %reduce-scatter.12.cloned.1.call-done = bf16[32,256]{1,0:T(8,128)(2,1)} async-done(((bf16[512,256]{1,0:T(8,128)(2,1)}), bf16[32,256]{1,0:T(8,128)(2,1)}) %reduce-scatter.12.cloned.1.call-update) | async-done | bytes 16400
  322.7 4.5 collective-permute-start.20
  327.3 4.9 collective-permute-start.23
  332.2 3.0 collective-permute-start.22
  339.8 6.8 %collective-permute-done.21 = bf16[128,256]{0,1:T(8,128)(2,1)S(1)} collective-permute-done((bf16[128,256]{0,1:T(8,128)(2,1)S(1)}, bf16[128,256]{0,1:T(8,128)(2,1)S(1)}, u32[]{:S(2)}, u32[]{:S(2)}) %collective-permute-start.21) | collective-permute-done | bytes 65568 | tf_op jit(solution)/shard_map/ppermute | solution.py:13
  348.8 3.7 scatter_fusion.2
  359.1 3.3 collective-permute-start.26
  362.4 3.6 collective-permute-start.25
  366.0 7.3 %collective-permute-done.25 = bf16[128,256]{1,0:T(8,128)(2,1)S(1)} collective-permute-done((bf16[128,256]{1,0:T(8,128)(2,1)S(1)}, bf16[128,256]{1,0:T(8,128)(2,1)S(1)}, u32[]{:S(2)}, u32[]{:S(2)}) %collective-permute-start.25) | collective-permute-done | bytes 65568 | tf_op jit(solution)/shard_map/ppermute | solution.py:13
  373.4 3.8 fusion.56
  381.1 3.6 collective-permute-start.30
  384.7 3.4 collective-permute-start.29
  396.4 5.2 scatter_fusion.3
  405.4 3.7 collective-permute-start.32
  411.0 3.6 collective-permute-start.34
  416.8 7.8 %collective-permute-done.33 = bf16[128,256]{1,0:T(8,128)(2,1)S(1)} collective-permute-done((bf16[128,256]{1,0:T(8,128)(2,1)S(1)}, bf16[128,256]{1,0:T(8,128)(2,1)S(1)}, u32[]{:S(2)}, u32[]{:S(2)}) %collective-permute-start.33) | collective-permute-done | bytes 65568 | tf_op jit(solution)/shard_map/ppermute | solution.py:13
  424.9 14.3 %all_to_all.17 = bf16[16,32,256]{2,1,0:T(8,128)(2,1)S(1)} all-to-all(bf16[16,32,256]{2,1,0:T(8,128)(2,1)S(1)} %stack.254), channel_id=1, replica_groups=mesh['row'=16,'col'=16] {'col'}, dimensions={0} | all-to-all | bytes 524288 | tf_op jit(solution)/shard_map/all_to_all | solution.py:79
  440.4 5.0 fusion.4
  445.5 74.7 %reduce-scatter.14.cloned.1.call-done = bf16[32,256]{1,0:T(8,128)(2,1)} async-done(((bf16[512,256]{1,0:T(8,128)(2,1)}), bf16[32,256]{1,0:T(8,128)(2,1)}) %reduce-scatter.14.cloned.1.call-update) | async-done | bytes 16400
  522.0 4.5 collective-permute-start.36
  526.5 5.0 collective-permute-start.39
  531.5 3.0 collective-permute-start.38
  540.1 5.9 %collective-permute-done.37 = bf16[128,256]{0,1:T(8,128)(2,1)S(1)} collective-permute-done((bf16[128,256]{0,1:T(8,128)(2,1)S(1)}, bf16[128,256]{0,1:T(8,128)(2,1)S(1)}, u32[]{:S(2)}, u32[]{:S(2)}) %collective-permute-start.37) | collective-permute-done | bytes 65568 | tf_op jit(solution)/shard_map/ppermute | solution.py:13
  548.2 5.2 scatter_fusion.4
  (134 shorter events, 88.1 us)
Async XLA Ops:
  6.5 39.9 %copy-start = (bf16[16,32,512]{2,1,0:T(8,128)(2,1)S(1)}, bf16[16,32,512]{2,1,0:T(8,128)(2,1)}, u32[]{:S(2)}) copy-start(bf16[16,32,512]{2,1,0:T(8,128)(2,1)} %param.11) | copy-start | bytes 1572868
  6.5 120.9 %reduce-scatter.10.cloned.1.call-start = ((), (), s32[]{:S(2)}) async-start(), calls=%async_computation.6 | async-start | bytes 278528
  9.3 24.4 %copy-start.1 = (bf16[1,1,1536,32]{2,3,1,0:T(8,128)(2,1)S(1)}, bf16[1,1,1536,32]{2,3,1,0:T(8,128)(2,1)}, u32[]{:S(2)}) copy-start(bf16[1,1,1536,32]{2,3,1,0:T(8,128)(2,1)} %param.10) | copy-start | bytes 294916
  11.4 13.6 %collective-permute-start = (bf16[128,256]{1,0:T(8,128)(2,1)S(1)}, bf16[128,256]{1,0:T(8,128)(2,1)S(1)}, u32[]{:S(2)}, u32[]{:S(2)}) collective-permute-start(bf16[128,256]{1,0:T(8,128)(2,1)S(1)} %get-tuple-element.41), channel_id=1, source_target_pairs={{0,16},{16,32},{32,48},{48,64},{64,80},{80,96},{96,112},{112,128},... | collective-permute-start | bytes 196616 | tf_op jit(solution)/shard_map/ppermute | solution.py:13
  17.2 7.8 %collective-permute-start.3 = (bf16[128,256]{1,0:T(8,128)(2,1)S(1)}, bf16[128,256]{1,0:T(8,128)(2,1)S(1)}, u32[]{:S(2)}, u32[]{:S(2)}) collective-permute-start(bf16[128,256]{1,0:T(8,128)(2,1)S(1)} %get-tuple-element.42), channel_id=1, source_target_pairs={{1,0},{2,1},{3,2},{4,3},{5,4},{6,5},{7,6},{8,7},{9,8},{10,9},{11,1... | collective-permute-start | bytes 196616 | tf_op jit(solution)/shard_map/ppermute | solution.py:13
  20.1 5.0 collective-permute-start.2
  23.1 10.5 %collective-permute-start.1 = (bf16[128,256]{1,0:T(8,128)(2,1)S(1)}, bf16[128,256]{1,0:T(8,128)(2,1)S(1)}, u32[]{:S(2)}, u32[]{:S(2)}) collective-permute-start(bf16[128,256]{1,0:T(8,128)(2,1)S(1)} %get-tuple-element.44), channel_id=1, source_target_pairs={{16,0},{32,16},{48,32},{64,48},{80,64},{96,80},{112,96},{128,112},... | collective-permute-start | bytes 196616 | tf_op jit(solution)/shard_map/ppermute | solution.py:13
  47.7 273.2 %reduce-scatter.12.cloned.1.call-start = ((), (), s32[]{:S(2)}) async-start(), calls=%async_computation.7 | async-start | bytes 278528
  128.6 14.8 %collective-permute-start.4 = (bf16[128,256]{0,1:T(8,128)(2,1)S(1)}, bf16[128,256]{0,1:T(8,128)(2,1)S(1)}, u32[]{:S(2)}, u32[]{:S(2)}) collective-permute-start(bf16[128,256]{0,1:T(8,128)(2,1)S(1)} %get-tuple-element.21), channel_id=1, source_target_pairs={{0,16},{16,32},{32,48},{48,64},{64,80},{80,96},{96,112},{112,128},... | collective-permute-start | bytes 196616 | tf_op jit(solution)/shard_map/ppermute | solution.py:13
  132.9 10.5 %collective-permute-start.7 = (bf16[128,256]{0,1:T(8,128)(2,1)S(1)}, bf16[128,256]{0,1:T(8,128)(2,1)S(1)}, u32[]{:S(2)}, u32[]{:S(2)}) collective-permute-start(bf16[128,256]{0,1:T(8,128)(2,1)S(1)} %get-tuple-element.22), channel_id=1, source_target_pairs={{1,0},{2,1},{3,2},{4,3},{5,4},{6,5},{7,6},{8,7},{9,8},{10,9},{11,1... | collective-permute-start | bytes 196616 | tf_op jit(solution)/shard_map/ppermute | solution.py:13
  138.1 5.4 collective-permute-start.6
  141.1 11.2 %collective-permute-start.5 = (bf16[128,256]{0,1:T(8,128)(2,1)S(1)}, bf16[128,256]{0,1:T(8,128)(2,1)S(1)}, u32[]{:S(2)}, u32[]{:S(2)}) collective-permute-start(bf16[128,256]{0,1:T(8,128)(2,1)S(1)} %get-tuple-element.24), channel_id=1, source_target_pairs={{16,0},{32,16},{48,32},{64,48},{80,64},{96,80},{112,96},{128,112},... | collective-permute-start | bytes 196616 | tf_op jit(solution)/shard_map/ppermute | solution.py:13
  158.6 10.9 %collective-permute-start.8 = (bf16[128,256]{1,0:T(8,128)(2,1)S(1)}, bf16[128,256]{1,0:T(8,128)(2,1)S(1)}, u32[]{:S(2)}, u32[]{:S(2)}) collective-permute-start(bf16[128,256]{1,0:T(8,128)(2,1)S(1)} %get-tuple-element.37), channel_id=1, source_target_pairs={{0,16},{16,32},{32,48},{48,64},{64,80},{80,96},{96,112},{112,128},... | collective-permute-start | bytes 196616 | tf_op jit(solution)/shard_map/ppermute | solution.py:13
  160.6 9.0 %collective-permute-start.11 = (bf16[128,256]{1,0:T(8,128)(2,1)S(1)}, bf16[128,256]{1,0:T(8,128)(2,1)S(1)}, u32[]{:S(2)}, u32[]{:S(2)}) collective-permute-start(bf16[128,256]{1,0:T(8,128)(2,1)S(1)} %get-tuple-element.38), channel_id=1, source_target_pairs={{1,0},{2,1},{3,2},{4,3},{5,4},{6,5},{7,6},{8,7},{9,8},{10,9},{11,1... | collective-permute-start | bytes 196616 | tf_op jit(solution)/shard_map/ppermute | solution.py:13
  162.5 7.0 %collective-permute-start.10 = (bf16[128,256]{1,0:T(8,128)(2,1)S(1)}, bf16[128,256]{1,0:T(8,128)(2,1)S(1)}, u32[]{:S(2)}, u32[]{:S(2)}) collective-permute-start(bf16[128,256]{1,0:T(8,128)(2,1)S(1)} %get-tuple-element.39), channel_id=1, source_target_pairs={{0,1},{1,2},{2,3},{3,4},{4,5},{5,6},{6,7},{7,8},{8,9},{9,10},{10,1... | collective-permute-start | bytes 196616 | tf_op jit(solution)/shard_map/ppermute | solution.py:13
  166.2 10.6 %collective-permute-start.9 = (bf16[128,256]{1,0:T(8,128)(2,1)S(1)}, bf16[128,256]{1,0:T(8,128)(2,1)S(1)}, u32[]{:S(2)}, u32[]{:S(2)}) collective-permute-start(bf16[128,256]{1,0:T(8,128)(2,1)S(1)} %get-tuple-element.40), channel_id=1, source_target_pairs={{16,0},{32,16},{48,32},{64,48},{80,64},{96,80},{112,96},{128,112},... | collective-permute-start | bytes 196616 | tf_op jit(solution)/shard_map/ppermute | solution.py:13
  180.7 13.5 %collective-permute-start.12 = (bf16[128,256]{0,1:T(8,128)(2,1)S(1)}, bf16[128,256]{0,1:T(8,128)(2,1)S(1)}, u32[]{:S(2)}, u32[]{:S(2)}) collective-permute-start(bf16[128,256]{0,1:T(8,128)(2,1)S(1)} %get-tuple-element.17), channel_id=1, source_target_pairs={{0,16},{16,32},{32,48},{48,64},{64,80},{80,96},{96,112},{112,128},... | collective-permute-start | bytes 196616 | tf_op jit(solution)/shard_map/ppermute | solution.py:13
  182.6 11.6 %collective-permute-start.15 = (bf16[128,256]{0,1:T(8,128)(2,1)S(1)}, bf16[128,256]{0,1:T(8,128)(2,1)S(1)}, u32[]{:S(2)}, u32[]{:S(2)}) collective-permute-start(bf16[128,256]{0,1:T(8,128)(2,1)S(1)} %get-tuple-element.18), channel_id=1, source_target_pairs={{1,0},{2,1},{3,2},{4,3},{5,4},{6,5},{7,6},{8,7},{9,8},{10,9},{11,1... | collective-permute-start | bytes 196616 | tf_op jit(solution)/shard_map/ppermute | solution.py:13
  184.5 9.7 %collective-permute-start.14 = (bf16[128,256]{0,1:T(8,128)(2,1)S(1)}, bf16[128,256]{0,1:T(8,128)(2,1)S(1)}, u32[]{:S(2)}, u32[]{:S(2)}) collective-permute-start(bf16[128,256]{0,1:T(8,128)(2,1)S(1)} %get-tuple-element.19), channel_id=1, source_target_pairs={{0,1},{1,2},{2,3},{3,4},{4,5},{5,6},{6,7},{7,8},{8,9},{9,10},{10,1... | collective-permute-start | bytes 196616 | tf_op jit(solution)/shard_map/ppermute | solution.py:13
  188.2 9.6 %collective-permute-start.13 = (bf16[128,256]{0,1:T(8,128)(2,1)S(1)}, bf16[128,256]{0,1:T(8,128)(2,1)S(1)}, u32[]{:S(2)}, u32[]{:S(2)}) collective-permute-start(bf16[128,256]{0,1:T(8,128)(2,1)S(1)} %get-tuple-element.20), channel_id=1, source_target_pairs={{16,0},{32,16},{48,32},{64,48},{80,64},{96,80},{112,96},{128,112},... | collective-permute-start | bytes 196616 | tf_op jit(solution)/shard_map/ppermute | solution.py:13
  207.4 11.7 %collective-permute-start.16 = (bf16[128,256]{1,0:T(8,128)(2,1)S(1)}, bf16[128,256]{1,0:T(8,128)(2,1)S(1)}, u32[]{:S(2)}, u32[]{:S(2)}) collective-permute-start(bf16[128,256]{1,0:T(8,128)(2,1)S(1)} %get-tuple-element.33), channel_id=1, source_target_pairs={{0,16},{16,32},{32,48},{48,64},{64,80},{80,96},{96,112},{112,128},... | collective-permute-start | bytes 196616 | tf_op jit(solution)/shard_map/ppermute | solution.py:13
  210.0 9.1 %collective-permute-start.19 = (bf16[128,256]{1,0:T(8,128)(2,1)S(1)}, bf16[128,256]{1,0:T(8,128)(2,1)S(1)}, u32[]{:S(2)}, u32[]{:S(2)}) collective-permute-start(bf16[128,256]{1,0:T(8,128)(2,1)S(1)} %get-tuple-element.34), channel_id=1, source_target_pairs={{1,0},{2,1},{3,2},{4,3},{5,4},{6,5},{7,6},{8,7},{9,8},{10,9},{11,1... | collective-permute-start | bytes 196616 | tf_op jit(solution)/shard_map/ppermute | solution.py:13
  211.9 7.2 %collective-permute-start.18 = (bf16[128,256]{1,0:T(8,128)(2,1)S(1)}, bf16[128,256]{1,0:T(8,128)(2,1)S(1)}, u32[]{:S(2)}, u32[]{:S(2)}) collective-permute-start(bf16[128,256]{1,0:T(8,128)(2,1)S(1)} %get-tuple-element.35), channel_id=1, source_target_pairs={{0,1},{1,2},{2,3},{3,4},{4,5},{5,6},{6,7},{7,8},{8,9},{9,10},{10,1... | collective-permute-start | bytes 196616 | tf_op jit(solution)/shard_map/ppermute | solution.py:13
  215.6 9.9 %collective-permute-start.17 = (bf16[128,256]{1,0:T(8,128)(2,1)S(1)}, bf16[128,256]{1,0:T(8,128)(2,1)S(1)}, u32[]{:S(2)}, u32[]{:S(2)}) collective-permute-start(bf16[128,256]{1,0:T(8,128)(2,1)S(1)} %get-tuple-element.36), channel_id=1, source_target_pairs={{16,0},{32,16},{48,32},{64,48},{80,64},{96,80},{112,96},{128,112},... | collective-permute-start | bytes 196616 | tf_op jit(solution)/shard_map/ppermute | solution.py:13
  241.0 279.1 %reduce-scatter.14.cloned.1.call-start = ((), (), s32[]{:S(2)}) async-start(), calls=%async_computation.8 | async-start | bytes 278528
  322.7 17.0 %collective-permute-start.20 = (bf16[128,256]{0,1:T(8,128)(2,1)S(1)}, bf16[128,256]{0,1:T(8,128)(2,1)S(1)}, u32[]{:S(2)}, u32[]{:S(2)}) collective-permute-start(bf16[128,256]{0,1:T(8,128)(2,1)S(1)} %get-tuple-element.13), channel_id=1, source_target_pairs={{0,16},{16,32},{32,48},{48,64},{64,80},{80,96},{96,112},{112,128},... | collective-permute-start | bytes 196616 | tf_op jit(solution)/shard_map/ppermute | solution.py:13
  327.3 12.5 %collective-permute-start.23 = (bf16[128,256]{0,1:T(8,128)(2,1)S(1)}, bf16[128,256]{0,1:T(8,128)(2,1)S(1)}, u32[]{:S(2)}, u32[]{:S(2)}) collective-permute-start(bf16[128,256]{0,1:T(8,128)(2,1)S(1)} %get-tuple-element.14), channel_id=1, source_target_pairs={{1,0},{2,1},{3,2},{4,3},{5,4},{6,5},{7,6},{8,7},{9,8},{10,9},{11,1... | collective-permute-start | bytes 196616 | tf_op jit(solution)/shard_map/ppermute | solution.py:13
  332.2 7.6 %collective-permute-start.22 = (bf16[128,256]{0,1:T(8,128)(2,1)S(1)}, bf16[128,256]{0,1:T(8,128)(2,1)S(1)}, u32[]{:S(2)}, u32[]{:S(2)}) collective-permute-start(bf16[128,256]{0,1:T(8,128)(2,1)S(1)} %get-tuple-element.15), channel_id=1, source_target_pairs={{0,1},{1,2},{2,3},{3,4},{4,5},{5,6},{6,7},{7,8},{8,9},{9,10},{10,1... | collective-permute-start | bytes 196616 | tf_op jit(solution)/shard_map/ppermute | solution.py:13
  335.2 11.4 %collective-permute-start.21 = (bf16[128,256]{0,1:T(8,128)(2,1)S(1)}, bf16[128,256]{0,1:T(8,128)(2,1)S(1)}, u32[]{:S(2)}, u32[]{:S(2)}) collective-permute-start(bf16[128,256]{0,1:T(8,128)(2,1)S(1)} %get-tuple-element.16), channel_id=1, source_target_pairs={{16,0},{32,16},{48,32},{64,48},{80,64},{96,80},{112,96},{128,112},... | collective-permute-start | bytes 196616 | tf_op jit(solution)/shard_map/ppermute | solution.py:13
  354.9 11.1 %collective-permute-start.24 = (bf16[128,256]{1,0:T(8,128)(2,1)S(1)}, bf16[128,256]{1,0:T(8,128)(2,1)S(1)}, u32[]{:S(2)}, u32[]{:S(2)}) collective-permute-start(bf16[128,256]{1,0:T(8,128)(2,1)S(1)} %get-tuple-element.29), channel_id=1, source_target_pairs={{0,16},{16,32},{32,48},{48,64},{64,80},{80,96},{96,112},{112,128},... | collective-permute-start | bytes 196616 | tf_op jit(solution)/shard_map/ppermute | solution.py:13
  356.8 9.2 %collective-permute-start.27 = (bf16[128,256]{1,0:T(8,128)(2,1)S(1)}, bf16[128,256]{1,0:T(8,128)(2,1)S(1)}, u32[]{:S(2)}, u32[]{:S(2)}) collective-permute-start(bf16[128,256]{1,0:T(8,128)(2,1)S(1)} %get-tuple-element.30), channel_id=1, source_target_pairs={{1,0},{2,1},{3,2},{4,3},{5,4},{6,5},{7,6},{8,7},{9,8},{10,9},{11,1... | collective-permute-start | bytes 196616 | tf_op jit(solution)/shard_map/ppermute | solution.py:13
  359.1 6.9 %collective-permute-start.26 = (bf16[128,256]{1,0:T(8,128)(2,1)S(1)}, bf16[128,256]{1,0:T(8,128)(2,1)S(1)}, u32[]{:S(2)}, u32[]{:S(2)}) collective-permute-start(bf16[128,256]{1,0:T(8,128)(2,1)S(1)} %get-tuple-element.31), channel_id=1, source_target_pairs={{0,1},{1,2},{2,3},{3,4},{4,5},{5,6},{6,7},{7,8},{8,9},{9,10},{10,1... | collective-permute-start | bytes 196616 | tf_op jit(solution)/shard_map/ppermute | solution.py:13
  362.4 11.0 %collective-permute-start.25 = (bf16[128,256]{1,0:T(8,128)(2,1)S(1)}, bf16[128,256]{1,0:T(8,128)(2,1)S(1)}, u32[]{:S(2)}, u32[]{:S(2)}) collective-permute-start(bf16[128,256]{1,0:T(8,128)(2,1)S(1)} %get-tuple-element.32), channel_id=1, source_target_pairs={{16,0},{32,16},{48,32},{64,48},{80,64},{96,80},{112,96},{128,112},... | collective-permute-start | bytes 196616 | tf_op jit(solution)/shard_map/ppermute | solution.py:13
  377.2 14.5 %collective-permute-start.28 = (bf16[128,256]{0,1:T(8,128)(2,1)S(1)}, bf16[128,256]{0,1:T(8,128)(2,1)S(1)}, u32[]{:S(2)}, u32[]{:S(2)}) collective-permute-start(bf16[128,256]{0,1:T(8,128)(2,1)S(1)} %get-tuple-element.9), channel_id=1, source_target_pairs={{0,16},{16,32},{32,48},{48,64},{64,80},{80,96},{96,112},{112,128},... | collective-permute-start | bytes 196616 | tf_op jit(solution)/shard_map/ppermute | solution.py:13
  379.1 12.6 %collective-permute-start.31 = (bf16[128,256]{0,1:T(8,128)(2,1)S(1)}, bf16[128,256]{0,1:T(8,128)(2,1)S(1)}, u32[]{:S(2)}, u32[]{:S(2)}) collective-permute-start(bf16[128,256]{0,1:T(8,128)(2,1)S(1)} %get-tuple-element.10), channel_id=1, source_target_pairs={{1,0},{2,1},{3,2},{4,3},{5,4},{6,5},{7,6},{8,7},{9,8},{10,9},{11,1... | collective-permute-start | bytes 196616 | tf_op jit(solution)/shard_map/ppermute | solution.py:13
  381.1 10.6 %collective-permute-start.30 = (bf16[128,256]{0,1:T(8,128)(2,1)S(1)}, bf16[128,256]{0,1:T(8,128)(2,1)S(1)}, u32[]{:S(2)}, u32[]{:S(2)}) collective-permute-start(bf16[128,256]{0,1:T(8,128)(2,1)S(1)} %get-tuple-element.11), channel_id=1, source_target_pairs={{0,1},{1,2},{2,3},{3,4},{4,5},{5,6},{6,7},{7,8},{8,9},{9,10},{10,1... | collective-permute-start | bytes 196616 | tf_op jit(solution)/shard_map/ppermute | solution.py:13
  384.7 9.5 %collective-permute-start.29 = (bf16[128,256]{0,1:T(8,128)(2,1)S(1)}, bf16[128,256]{0,1:T(8,128)(2,1)S(1)}, u32[]{:S(2)}, u32[]{:S(2)}) collective-permute-start(bf16[128,256]{0,1:T(8,128)(2,1)S(1)} %get-tuple-element.12), channel_id=1, source_target_pairs={{16,0},{32,16},{48,32},{64,48},{80,64},{96,80},{112,96},{128,112},... | collective-permute-start | bytes 196616 | tf_op jit(solution)/shard_map/ppermute | solution.py:13
  405.4 11.3 %collective-permute-start.32 = (bf16[128,256]{1,0:T(8,128)(2,1)S(1)}, bf16[128,256]{1,0:T(8,128)(2,1)S(1)}, u32[]{:S(2)}, u32[]{:S(2)}) collective-permute-start(bf16[128,256]{1,0:T(8,128)(2,1)S(1)} %get-tuple-element.25), channel_id=1, source_target_pairs={{0,16},{16,32},{32,48},{48,64},{64,80},{80,96},{96,112},{112,128},... | collective-permute-start | bytes 196616 | tf_op jit(solution)/shard_map/ppermute | solution.py:13
  409.1 7.7 %collective-permute-start.35 = (bf16[128,256]{1,0:T(8,128)(2,1)S(1)}, bf16[128,256]{1,0:T(8,128)(2,1)S(1)}, u32[]{:S(2)}, u32[]{:S(2)}) collective-permute-start(bf16[128,256]{1,0:T(8,128)(2,1)S(1)} %get-tuple-element.26), channel_id=1, source_target_pairs={{1,0},{2,1},{3,2},{4,3},{5,4},{6,5},{7,6},{8,7},{9,8},{10,9},{11,1... | collective-permute-start | bytes 196616 | tf_op jit(solution)/shard_map/ppermute | solution.py:13
  411.0 5.8 %collective-permute-start.34 = (bf16[128,256]{1,0:T(8,128)(2,1)S(1)}, bf16[128,256]{1,0:T(8,128)(2,1)S(1)}, u32[]{:S(2)}, u32[]{:S(2)}) collective-permute-start(bf16[128,256]{1,0:T(8,128)(2,1)S(1)} %get-tuple-element.27), channel_id=1, source_target_pairs={{0,1},{1,2},{2,3},{3,4},{4,5},{5,6},{6,7},{7,8},{8,9},{9,10},{10,1... | collective-permute-start | bytes 196616 | tf_op jit(solution)/shard_map/ppermute | solution.py:13
  414.7 9.9 %collective-permute-start.33 = (bf16[128,256]{1,0:T(8,128)(2,1)S(1)}, bf16[128,256]{1,0:T(8,128)(2,1)S(1)}, u32[]{:S(2)}, u32[]{:S(2)}) collective-permute-start(bf16[128,256]{1,0:T(8,128)(2,1)S(1)} %get-tuple-element.28), channel_id=1, source_target_pairs={{16,0},{32,16},{48,32},{64,48},{80,64},{96,80},{112,96},{128,112},... | collective-permute-start | bytes 196616 | tf_op jit(solution)/shard_map/ppermute | solution.py:13
  424.6 14.6 %copy-start.2 = (bf16[4,128,256]{2,1,0:T(8,128)(2,1)}, bf16[4,128,256]{2,1,0:T(8,128)(2,1)S(1)}, u32[]{:S(2)}) copy-start(bf16[4,128,256]{2,1,0:T(8,128)(2,1)S(1)} %pad_maximum_fusion.13) | copy-start | bytes 786436
  522.0 18.0 %collective-permute-start.36 = (bf16[128,256]{0,1:T(8,128)(2,1)S(1)}, bf16[128,256]{0,1:T(8,128)(2,1)S(1)}, u32[]{:S(2)}, u32[]{:S(2)}) collective-permute-start(bf16[128,256]{0,1:T(8,128)(2,1)S(1)} %get-tuple-element.5), channel_id=1, source_target_pairs={{0,16},{16,32},{32,48},{48,64},{64,80},{80,96},{96,112},{112,128},... | collective-permute-start | bytes 196616 | tf_op jit(solution)/shard_map/ppermute | solution.py:13
  526.5 13.5 %collective-permute-start.39 = (bf16[128,256]{0,1:T(8,128)(2,1)S(1)}, bf16[128,256]{0,1:T(8,128)(2,1)S(1)}, u32[]{:S(2)}, u32[]{:S(2)}) collective-permute-start(bf16[128,256]{0,1:T(8,128)(2,1)S(1)} %get-tuple-element.6), channel_id=1, source_target_pairs={{1,0},{2,1},{3,2},{4,3},{5,4},{6,5},{7,6},{8,7},{9,8},{10,9},{11,1... | collective-permute-start | bytes 196616 | tf_op jit(solution)/shard_map/ppermute | solution.py:13
  531.5 8.5 %collective-permute-start.38 = (bf16[128,256]{0,1:T(8,128)(2,1)S(1)}, bf16[128,256]{0,1:T(8,128)(2,1)S(1)}, u32[]{:S(2)}, u32[]{:S(2)}) collective-permute-start(bf16[128,256]{0,1:T(8,128)(2,1)S(1)} %get-tuple-element.7), channel_id=1, source_target_pairs={{0,1},{1,2},{2,3},{3,4},{4,5},{5,6},{6,7},{7,8},{8,9},{9,10},{10,1... | collective-permute-start | bytes 196616 | tf_op jit(solution)/shard_map/ppermute | solution.py:13
  534.5 11.4 %collective-permute-start.37 = (bf16[128,256]{0,1:T(8,128)(2,1)S(1)}, bf16[128,256]{0,1:T(8,128)(2,1)S(1)}, u32[]{:S(2)}, u32[]{:S(2)}) collective-permute-start(bf16[128,256]{0,1:T(8,128)(2,1)S(1)} %get-tuple-element.8), channel_id=1, source_target_pairs={{16,0},{32,16},{48,32},{64,48},{80,64},{96,80},{112,96},{128,112},... | collective-permute-start | bytes 196616 | tf_op jit(solution)/shard_map/ppermute | solution.py:13
Sparse Core Ops, SparseCore 0:
  47.8 79.5 reduce-scatter.9
  241.2 79.6 reduce-scatter.11
  440.5 79.5 reduce-scatter.13
